TPU v7x, 512 devices: a whole 4x4x16 slice. The times are simulated.
512 devices in a mesh: segment: 4 (over x), expert: 64 (over y, z), dp: 2 (over core).
Axes of the slice: x: 4, y: 4, z: 16, core: 2. Of those that a mesh axis runs over, the one named last changes fastest.
Arguments:
- act_in: bfloat16 [4, 14336, 2048], P('segment', ('expert', 'dp')), may hold values from -6 to 6
- stash_in: bfloat16 [4, 14336, 2048], P('segment', ('expert', 'dp')), may hold values from -6 to 6
- grad_in: bfloat16 [4, 14336, 2048], P('segment', ('expert', 'dp')), may hold values from -6 to 6
- route_a: int32 [4, 14336, 2], P('segment', ('expert', 'dp')), may hold values from 0 to 31, all different within a row; in each aligned block of 112 rows (0 to 111, 112 to 223, ..., all dimensions but the last counted through in order) at most 8 rows name the same one
- route_b: int32 [4, 14336, 2], P('segment', ('expert', 'dp')), may hold values from 0 to 31, all different within a row; in each aligned block of 112 rows (0 to 111, 112 to 223, ..., all dimensions but the last counted through in order) at most 8 rows name the same one
- norm_gain: float32 [4, 2048], P('segment'), may hold values from 0.5 to 1.5
- router: bfloat16 [4, 32, 2048], P('segment'), may hold values from -0.5 to 0.5
- gate_weight: bfloat16 [4, 64, 352, 2048], P('segment', 'expert', 'dp'), may hold values from -0.125 to 0.125
- up_weight: bfloat16 [4, 64, 352, 2048], P('segment', 'expert', 'dp'), may hold values from -0.125 to 0.125
- down_weight: bfloat16 [4, 64, 352, 2048], P('segment', 'expert', 'dp'), may hold values from -0.21875 to 0.21875
Outputs:
- next_act: bfloat16 [4, 14336, 2048], P('segment', ('expert', 'dp'))
- prev_grad: bfloat16 [4, 14336, 2048], P('segment', ('expert', 'dp'))
- router_grad: float32 [4, 32, 2048], P('segment')
- gain_grad: float32 [4, 2048], P('segment')
Inputs may be any that keep to these rules, and one draw needn't show every extreme that they name: `route_a`: each row names two different experts. In each aligned block of 112 rows (the tokens of one device) no expert is named more than 8 times, a bound that some block reaches in every draw. `route_b`: as route_a.
All inputs are finite; a program needn't handle non-finite values.
Results may differ from a plain program's by a relative error of at most 0.011.
Values may be sent and summed in bfloat16 or wider, within the bound.
A program may use at most 64 MiB of HBM per device.

v0:
```python
import jax
import jax.numpy as jnp
from jax import lax
from jax.sharding import PartitionSpec as P

EPS = 1e-06


def partner_2(shard, axis, stride):
    return lax.ppermute(shard, axis, [(i, i ^ 1 << stride) for i in range(lax.axis_size(axis))])


def from_behind(value, axis, steps):
    count = lax.axis_size(axis)
    pairs = [(source, (source + steps) % count) for source in range(count)]
    return lax.ppermute(value, axis, pairs)


def order_halves(own_part, far_part, parity):
    low_half = jnp.where(parity == 0, own_part, far_part)
    high_half = jnp.where(parity == 0, far_part, own_part)
    return jnp.stack([low_half, high_half])


def prepare(x_block, route, gain, router_w):
    x_float = x_block.astype(jnp.float32)
    inv_rms = lax.rsqrt(jnp.mean(x_float * x_float, -1, keepdims=True) + EPS)
    normed = (x_float * inv_rms * gain[None, :]).astype(jnp.bfloat16)
    logits = jnp.einsum("td,ed->te", normed, router_w, preferred_element_type=jnp.float32)
    chosen_mask = route[:, :, None] == jnp.arange(router_w.shape[0], dtype=jnp.int32)[None, None, :]
    chosen = jnp.sum(jnp.where(chosen_mask, logits[:, None, :], 0.0), -1)
    weight_one = jax.nn.sigmoid(chosen[:, 0] - chosen[:, 1])
    weight_two = jax.nn.sigmoid(chosen[:, 1] - chosen[:, 0])
    return (x_float, inv_rms, normed, chosen_mask, weight_one, weight_two)


def route_slots(route, experts, capacity, owners, offset):
    expert_ids = route.reshape(-1)
    onehot = (expert_ids[:, None] == jnp.arange(experts, dtype=jnp.int32)[None, :]).astype(
        jnp.int32
    )
    rank = jnp.sum(jnp.cumsum(onehot, axis=0) * onehot, -1) - 1
    position = (2 * expert_ids + (rank + offset) % 2) * capacity + rank // 2
    pair_count = expert_ids.shape[0]
    slot_pair = jnp.full((owners * capacity,), pair_count, jnp.int32)
    slot_pair = slot_pair.at[position].set(jnp.arange(pair_count, dtype=jnp.int32))
    return (position, slot_pair)


def pad_rows(rows):
    return jnp.concatenate([rows, jnp.zeros((1, rows.shape[1]), rows.dtype)], 0)


def body(
    act_in,
    stash_in,
    grad_in,
    route_a,
    route_b,
    norm_gain,
    router,
    gate_weight,
    up_weight,
    down_weight,
):
    parity = lax.axis_index("expert") % 2
    quarters = (gate_weight[0, 0], up_weight[0, 0], down_weight[0, 0])
    halves = (
        lax.all_gather(quarters[0], "dp", axis=0, tiled=True),
        lax.all_gather(quarters[1], "dp", axis=0, tiled=True),
        lax.all_gather(quarters[2], "dp", axis=0, tiled=True),
    )
    partner = partner_2((halves[0], halves[1], halves[2]), "expert", 0)
    weights = tuple((order_halves(halves[which], partner[which], parity) for which in range(3)))
    gate_full, up_full, down_full = weights
    gain = norm_gain[0]
    router_w = router[0]
    experts = router_w.shape[0]
    width = act_in.shape[2]
    tokens = act_in.shape[1]
    owners = lax.axis_size("expert")
    most_rows = 2 * min(tokens // experts + 1, tokens // 2)
    capacity = (most_rows + 1) // 2

    def expert_forward(block_rows):
        flat_rows = block_rows.reshape(-1, width)
        gate_val = jnp.einsum(
            "rd,phd->rph", flat_rows, gate_full, preferred_element_type=jnp.float32
        )
        up_val = jnp.einsum("rd,phd->rph", flat_rows, up_full, preferred_element_type=jnp.float32)
        hidden = (jax.nn.silu(gate_val) * up_val).astype(jnp.bfloat16)
        output = jnp.einsum("rph,phd->rd", hidden, down_full, preferred_element_type=jnp.float32)
        return (output.astype(jnp.bfloat16).reshape(block_rows.shape), gate_val, up_val)

    x_float, inv_rms, normed, chosen_mask, weight_one, weight_two = prepare(
        act_in[0], route_a[0], gain, router_w
    )
    position, slot_pair = route_slots(route_a[0], experts, capacity, owners, parity)
    send_rows = jnp.take(pad_rows(normed), slot_pair // 2, axis=0).reshape(owners, capacity, width)
    output, gate_val, up_val = expert_forward(
        lax.all_to_all(send_rows, "expert", split_axis=0, concat_axis=0, tiled=True)
    )
    returned = lax.all_to_all(output, "expert", split_axis=0, concat_axis=0, tiled=True)
    pair_out = (
        jnp.take(returned.reshape(-1, width), position, axis=0)
        .reshape(tokens, 2, width)
        .astype(jnp.float32)
    )
    mixed = x_float + weight_one[:, None] * pair_out[:, 0] + weight_two[:, None] * pair_out[:, 1]
    next_act = from_behind(mixed.astype(jnp.bfloat16), "segment", 1)
    x_float, inv_rms, normed, chosen_mask, weight_one, weight_two = prepare(
        stash_in[0], route_b[0], gain, router_w
    )
    position, slot_pair = route_slots(route_b[0], experts, capacity, owners, parity)
    send_rows = jnp.take(pad_rows(normed), slot_pair // 2, axis=0).reshape(owners, capacity, width)
    received = lax.all_to_all(send_rows, "expert", split_axis=0, concat_axis=0, tiled=True)
    expert_out, gate_val, up_val = expert_forward(received)
    returned = lax.all_to_all(expert_out, "expert", split_axis=0, concat_axis=0, tiled=True)
    pair_out = (
        jnp.take(returned.reshape(-1, width), position, axis=0)
        .reshape(tokens, 2, width)
        .astype(jnp.float32)
    )
    out_grad = grad_in[0].astype(jnp.float32)
    dot_one = jnp.sum(out_grad * pair_out[:, 0], -1)
    dot_two = jnp.sum(out_grad * pair_out[:, 1], -1)
    logit_grad = weight_one * weight_two * (dot_one - dot_two)
    signs = chosen_mask[:, 0].astype(jnp.float32) - chosen_mask[:, 1].astype(jnp.float32)
    dlogits = (logit_grad[:, None] * signs).astype(jnp.bfloat16)
    pair_grad = jnp.stack(
        [weight_one[:, None] * out_grad, weight_two[:, None] * out_grad], 1
    ).astype(jnp.bfloat16)
    send_grads = jnp.take(
        pad_rows(pair_grad.reshape(tokens * 2, width)), slot_pair, axis=0
    ).reshape(owners, capacity, width)
    grad_rows = lax.all_to_all(
        send_grads, "expert", split_axis=0, concat_axis=0, tiled=True
    ).reshape(-1, width)
    grad_hidden = jnp.einsum(
        "rd,phd->rph", grad_rows, down_full, preferred_element_type=jnp.float32
    )
    sigma = jax.nn.sigmoid(gate_val)
    grad_gate = (grad_hidden * up_val * sigma * (1.0 + gate_val * (1.0 - sigma))).astype(
        jnp.bfloat16
    )
    grad_up = (grad_hidden * gate_val * sigma).astype(jnp.bfloat16)
    grad_normed_rows = jnp.einsum(
        "rph,phd->rd", grad_gate, gate_full, preferred_element_type=jnp.float32
    )
    grad_normed_rows = grad_normed_rows + jnp.einsum(
        "rph,phd->rd", grad_up, up_full, preferred_element_type=jnp.float32
    )
    grad_normed_rows = grad_normed_rows.astype(jnp.bfloat16).reshape(owners, capacity, width)
    grad_back = lax.all_to_all(grad_normed_rows, "expert", split_axis=0, concat_axis=0, tiled=True)
    pair_back = (
        jnp.take(grad_back.reshape(-1, width), position, axis=0)
        .reshape(tokens, 2, width)
        .astype(jnp.float32)
    )
    dnormed = (
        pair_back[:, 0]
        + pair_back[:, 1]
        + jnp.dot(dlogits, router_w, preferred_element_type=jnp.float32)
    )
    router_term = jnp.einsum("te,td->ed", dlogits, normed, preferred_element_type=jnp.float32)
    gain_term = jnp.sum(dnormed * x_float * inv_rms, 0)
    router_sum, gain_sum = lax.psum((router_term, gain_term), ("expert", "dp"))
    blocks = lax.axis_size("expert") * lax.axis_size("dp")
    dxn = dnormed * gain[None, :]
    input_grad = (
        out_grad + inv_rms * dxn - x_float * inv_rms**3 * jnp.mean(dxn * x_float, -1, keepdims=True)
    )
    prev_grad = from_behind(input_grad.astype(jnp.bfloat16), "segment", -1)
    return (next_act[None], prev_grad[None], (router_sum / blocks)[None], (gain_sum / blocks)[None])


def solution(mesh):
    in_specs = (
        P("segment", ("expert", "dp"), None),
        P("segment", ("expert", "dp"), None),
        P("segment", ("expert", "dp"), None),
        P("segment", ("expert", "dp"), None),
        P("segment", ("expert", "dp"), None),
        P("segment", None),
        P("segment", None, None),
        P("segment", "expert", "dp", None),
        P("segment", "expert", "dp", None),
        P("segment", "expert", "dp", None),
    )
    out_specs = (
        P("segment", ("expert", "dp"), None),
        P("segment", ("expert", "dp"), None),
        P("segment", None, None),
        P("segment", None),
    )
    return jax.shard_map(body, mesh=mesh, in_specs=in_specs, out_specs=out_specs, check_vma=False)
```

profile of v0, /device:TPU:1, one launch (start us, length us, event | category | flops | bytes accessed | tf_op | source)
XLA Modules:
  0.0 1096.4 jit_solution(4540719086788931568)
XLA Ops:
  8.7 0.8 copy.18
  16.1 1.3 scatter_custom_fusion.1
  17.4 1.4 gather_fusion.3
  19.0 1.3 reshape.523
  20.2 19.3 %all-to-all-start.3 = ((bf16[64,4,2048]{2,1,0:T(4,128)(2,1)}), bf16[64,4,2048]{2,1,0:T(4,128)(2,1)S(1)}, u32[]{:S(2)}, u32[]{:S(2)}) async-start(bf16[64,4,2048]{2,1,0:T(4,128)(2,1)} %reshape.523), calls=%async_computation.3 | async-start | bytes 2097152 | tf_op jit(solution)/shard_map/all_to_all | solution.py:116
  40.3 2.9 collective-permute-start
  43.2 17.3 %all-gather.9.cloned.1.call-done = bf16[1,1,352,2048]{3,2,1,0:T(8,128)(2,1)} async-done(((bf16[1,1,176,2048]{3,2,1,0:T(8,128)(2,1)}), bf16[1,1,352,2048]{3,2,1,0:T(8,128)(2,1)}) %all-gather.9.cloned.1.call-update) | async-done | bytes 1441808 | tf_op jit(solution)/shard_map/all_gather | solution.py:70
  60.5 2.2 collective-permute-start.1
  62.7 21.4 %all-gather.11.cloned.1.call-done = bf16[1,1,352,2048]{3,2,1,0:T(8,128)(2,1)} async-done(((bf16[1,1,176,2048]{3,2,1,0:T(8,128)(2,1)}), bf16[1,1,352,2048]{3,2,1,0:T(8,128)(2,1)}) %all-gather.11.cloned.1.call-update) | async-done | bytes 1441808 | tf_op jit(solution)/shard_map/all_gather | solution.py:71
  84.1 2.2 collective-permute-start.2
  86.3 30.3 %collective-permute-done = bf16[352,2048]{1,0:T(8,128)(2,1)} collective-permute-done((bf16[352,2048]{1,0:T(8,128)(2,1)}, bf16[352,2048]{1,0:T(8,128)(2,1)}, u32[]{:S(2)}, u32[]{:S(2)}) %collective-permute-start) | collective-permute-done | bytes 1441824 | tf_op jit(solution)/shard_map/ppermute | solution.py:10
  116.5 3.1 select_bitcast_fusion.5
  119.6 27.8 %collective-permute-done.1 = bf16[352,2048]{1,0:T(8,128)(2,1)} collective-permute-done((bf16[352,2048]{1,0:T(8,128)(2,1)}, bf16[352,2048]{1,0:T(8,128)(2,1)}, u32[]{:S(2)}, u32[]{:S(2)}) %collective-permute-start.1) | collective-permute-done | bytes 1441824 | tf_op jit(solution)/shard_map/ppermute | solution.py:10
  147.4 3.2 select_bitcast_fusion.3
  150.6 27.7 %collective-permute-done.2 = bf16[352,2048]{1,0:T(8,128)(2,1)} collective-permute-done((bf16[352,2048]{1,0:T(8,128)(2,1)}, bf16[352,2048]{1,0:T(8,128)(2,1)}, u32[]{:S(2)}, u32[]{:S(2)}) %collective-permute-start.2) | collective-permute-done | bytes 1441824 | tf_op jit(solution)/shard_map/ppermute | solution.py:10
  178.3 3.2 select_bitcast_fusion.1
  181.5 1.1 reshape.624
  182.6 2.8 fusion.45
  185.4 0.9 fusion.43
  187.7 1.1 fusion.3
  188.8 1.2 reshape.527
  190.1 15.0 %all-to-all-start.5 = ((bf16[64,4,2048]{2,1,0:T(4,128)(2,1)}), bf16[64,4,2048]{2,1,0:T(4,128)(2,1)S(1)}, u32[]{:S(2)}, u32[]{:S(2)}) async-start(bf16[64,4,2048]{2,1,0:T(4,128)(2,1)} %reshape.527), calls=%async_computation.5 | async-start | bytes 2097152 | tf_op jit(solution)/shard_map/all_to_all | solution.py:118
  205.7 49.7 %all-to-all-done.5 = bf16[64,4,2048]{2,1,0:T(4,128)(2,1)S(1)} async-done(((bf16[64,4,2048]{2,1,0:T(4,128)(2,1)}), bf16[64,4,2048]{2,1,0:T(4,128)(2,1)S(1)}, u32[]{:S(2)}, u32[]{:S(2)}) %all-to-all-start.5) | async-done | bytes 1048608 | tf_op jit(solution)/shard_map/all_to_all | solution.py:118
  255.7 1.3 gather_fusion.5
  256.9 1.4 select_convert_fusion
  258.3 2.4 reshape.537
  260.7 1.4 fusion.96
  263.6 0.9 copy.28
  265.0 1.4 gather_fusion
  267.4 60.5 %all_to_all.30 = bf16[64,4,2048]{2,1,0:T(4,128)(2,1)S(1)} all-to-all(bf16[64,4,2048]{2,1,0:T(4,128)(2,1)S(1)} %broadcast_select_fusion.2), channel_id=1, replica_groups=mesh['segment'=4,'expert'=64,'dp'=2] {'expert'}, dimensions={0} | all-to-all | bytes 2097152 | tf_op jit(solution)/shard_map/all_to_all | solution.py:136
  327.9 1.1 reshape.623
  329.0 2.8 fusion.42
  331.9 1.1 convolution_bitcast_fusion.1
  333.8 1.1 fusion.1
  335.0 1.3 reshape.525
  336.2 10.1 all-to-all-start.4
  346.4 1.4 scatter_custom_fusion
  347.8 48.8 %all-to-all-done.4 = bf16[64,4,2048]{2,1,0:T(4,128)(2,1)S(1)} async-done(((bf16[64,4,2048]{2,1,0:T(4,128)(2,1)}), bf16[64,4,2048]{2,1,0:T(4,128)(2,1)S(1)}, u32[]{:S(2)}, u32[]{:S(2)}) %all-to-all-start.4) | async-done | bytes 1048608 | tf_op jit(solution)/shard_map/all_to_all | solution.py:154
  396.9 1.3 gather_fusion.4
  398.2 1.5 select_convert_fusion.1
  399.7 2.4 reshape.536
  402.1 1.4 fusion.95
  403.5 0.8 fusion.36
  404.7 1.2 fusion.29
  405.9 1.4 gather_fusion.1
  407.8 60.2 %all_to_all.31 = bf16[64,4,2048]{2,1,0:T(4,128)(2,1)S(1)} all-to-all(bf16[64,4,2048]{2,1,0:T(4,128)(2,1)S(1)} %reshape.516), channel_id=1, replica_groups=mesh['segment'=4,'expert'=64,'dp'=2] {'expert'}, dimensions={0} | all-to-all | bytes 2097152 | tf_op jit(solution)/shard_map/all_to_all | solution.py:101
  468.1 1.2 reshape.621
  469.2 4.0 fusion.44
  473.3 7.1 fusion.2
  480.3 2.2 reshape.518
  482.6 10.2 all-to-all-start.1
  493.3 1.0 fusion.61
  494.4 4.4 collective-permute-start.4
  498.8 44.7 %all-to-all-done.1 = bf16[64,4,2048]{2,1,0:T(4,128)(2,1)S(1)} async-done(((bf16[64,4,2048]{2,1,0:T(4,128)(2,1)}), bf16[64,4,2048]{2,1,0:T(4,128)(2,1)S(1)}, u32[]{:S(2)}, u32[]{:S(2)}) %all-to-all-start.1) | async-done | bytes 1048608 | tf_op jit(solution)/shard_map/all_to_all | solution.py:103
  543.8 1.3 gather_fusion.2
  545.0 1.5 select_convert_fusion.2
  546.5 2.4 reshape.531
  548.9 1.4 fusion.97
  550.3 0.9 fusion.21
  551.2 3.1 collective-permute-start.3
  554.4 278.7 %all-reduce.7.cloned.1.call-done = f32[32,2048]{1,0:T(8,128)} async-done(((f32[32,2048]{1,0:T(8,128)}), f32[32,2048]{1,0:T(8,128)}) %all-reduce.7.cloned.1.call-update) | async-done | bytes 262160 | tf_op jit(solution)/shard_map/psum | solution.py:167
  833.1 1.7 multiply_bitcast_fusion
  834.8 251.6 %psum.15 = f32[2048]{0:T(1024)S(1)} all-reduce(f32[2048]{0:T(1024)S(1)} %get-tuple-element.6), channel_id=1, replica_groups=mesh['segment'=4,'expert'=64,'dp'=2] {'expert','dp'}, use_global_device_ids=true, to_apply=%region_17.20 | all-reduce | flops 2048 | bytes 16384 | tf_op jit(solution)/shard_map/psum | solution.py:167
  1087.8 1.8 copy.74
  (140 shorter events, 18.1 us)
Async XLA Ops:
  7.2 198.1 %copy-start = (bf16[1,32,2048]{2,1,0:T(8,128)(2,1)S(1)}, bf16[1,32,2048]{2,1,0:T(8,128)(2,1)}, u32[]{:S(2)}) copy-start(bf16[1,32,2048]{2,1,0:T(8,128)(2,1)} %param.20) | copy-start | bytes 393220
  7.2 7.2 copy-start.2
  7.2 7.4 copy-start.1
  7.2 8.1 copy-start.20
  7.2 33.0 %all-gather.7.cloned.1.call-start = ((), (), s32[]{:S(2)}) async-start(), calls=%async_computation.7 | async-start | bytes 2162688 | tf_op jit(solution)/shard_map/all_gather | solution.py:69
  7.9 52.6 %all-gather.9.cloned.1.call-start = ((), (), s32[]{:S(2)}) async-start(), calls=%async_computation.8 | async-start | bytes 2162688 | tf_op jit(solution)/shard_map/all_gather | solution.py:70
  20.2 161.3 %all-to-all-start.3 = ((bf16[64,4,2048]{2,1,0:T(4,128)(2,1)}), bf16[64,4,2048]{2,1,0:T(4,128)(2,1)S(1)}, u32[]{:S(2)}, u32[]{:S(2)}) async-start(bf16[64,4,2048]{2,1,0:T(4,128)(2,1)} %reshape.523), calls=%async_computation.3 | async-start | bytes 2097152 | tf_op jit(solution)/shard_map/all_to_all | solution.py:116
  39.5 44.6 %all-gather.11.cloned.1.call-start = ((), (), s32[]{:S(2)}) async-start(), calls=%async_computation.9 | async-start | bytes 2162688 | tf_op jit(solution)/shard_map/all_gather | solution.py:71
  40.3 76.3 %collective-permute-start = (bf16[352,2048]{1,0:T(8,128)(2,1)}, bf16[352,2048]{1,0:T(8,128)(2,1)}, u32[]{:S(2)}, u32[]{:S(2)}) collective-permute-start(bf16[352,2048]{1,0:T(8,128)(2,1)} %bitcast.208), channel_id=1, source_target_pairs={{0,2},{2,0},{4,6},{6,4},{8,10},{10,8},{12,14},{14,12},{16,18},{18,... | collective-permute-start | bytes 4325384 | tf_op jit(solution)/shard_map/ppermute | solution.py:10
  60.5 86.9 %collective-permute-start.1 = (bf16[352,2048]{1,0:T(8,128)(2,1)}, bf16[352,2048]{1,0:T(8,128)(2,1)}, u32[]{:S(2)}, u32[]{:S(2)}) collective-permute-start(bf16[352,2048]{1,0:T(8,128)(2,1)} %bitcast.209), channel_id=1, source_target_pairs={{0,2},{2,0},{4,6},{6,4},{8,10},{10,8},{12,14},{14,12},{16,18},{18,... | collective-permute-start | bytes 4325384 | tf_op jit(solution)/shard_map/ppermute | solution.py:10
  84.1 94.3 %collective-permute-start.2 = (bf16[352,2048]{1,0:T(8,128)(2,1)}, bf16[352,2048]{1,0:T(8,128)(2,1)}, u32[]{:S(2)}, u32[]{:S(2)}) collective-permute-start(bf16[352,2048]{1,0:T(8,128)(2,1)} %bitcast.210), channel_id=1, source_target_pairs={{0,2},{2,0},{4,6},{6,4},{8,10},{10,8},{12,14},{14,12},{16,18},{18,... | collective-permute-start | bytes 4325384 | tf_op jit(solution)/shard_map/ppermute | solution.py:10
  86.3 61.2 %copy-start.17 = (bf16[1,1,352,2048]{3,2,1,0:T(8,128)(2,1)S(1)}, bf16[1,1,352,2048]{3,2,1,0:T(8,128)(2,1)}, u32[]{:S(2)}) copy-start(bf16[1,1,352,2048]{3,2,1,0:T(8,128)(2,1)} %all-gather.9.cloned.1.call-done) | copy-start | bytes 4325380
  119.6 62.9 %copy-start.6 = (bf16[1,352,2048]{2,1,0:T(8,128)(2,1)}, bf16[1,352,2048]{2,1,0:T(8,128)(2,1)S(1)}, u32[]{:S(2)}) copy-start(bf16[1,352,2048]{2,1,0:T(8,128)(2,1)S(1)} %get-tuple-element.21) | copy-start | bytes 4325380
  119.6 58.7 %copy-start.18 = (bf16[1,1,352,2048]{3,2,1,0:T(8,128)(2,1)S(1)}, bf16[1,1,352,2048]{3,2,1,0:T(8,128)(2,1)}, u32[]{:S(2)}) copy-start(bf16[1,1,352,2048]{3,2,1,0:T(8,128)(2,1)} %all-gather.11.cloned.1.call-done) | copy-start | bytes 4325380
  182.6 2.8 copy-start.10
  182.6 2.8 copy-start.12
  182.6 2.8 copy-start.19
  185.4 1.0 copy-start.25
  185.4 1.6 copy-start.14
  185.4 2.3 copy-start.16
  186.4 2.4 copy-start.27
  190.1 15.5 %copy-start.21 = (s32[1,112,2]{1,2,0:T(2,128)S(1)}, s32[1,112,2]{1,2,0:T(2,128)}, u32[]{:S(2)}) copy-start(s32[1,112,2]{1,2,0:T(2,128)} %param.18) | copy-start | bytes 2692
  190.1 65.3 %all-to-all-start.5 = ((bf16[64,4,2048]{2,1,0:T(4,128)(2,1)}), bf16[64,4,2048]{2,1,0:T(4,128)(2,1)S(1)}, u32[]{:S(2)}, u32[]{:S(2)}) async-start(bf16[64,4,2048]{2,1,0:T(4,128)(2,1)} %reshape.527), calls=%async_computation.5 | async-start | bytes 2097152 | tf_op jit(solution)/shard_map/all_to_all | solution.py:118
  260.7 1.4 copy-start.4
  267.4 61.6 %copy-start.15 = (bf16[1,352,2048]{2,1,0:T(8,128)(2,1)S(1)}, bf16[1,352,2048]{2,1,0:T(8,128)(2,1)}, u32[]{:S(2)}) copy-start(bf16[1,352,2048]{2,1,0:T(8,128)(2,1)} %get-tuple-element.25) | copy-start | bytes 4325380
  329.0 2.8 copy-start.11
  329.0 2.8 copy-start.13
  329.0 2.8 copy-start.26
  331.8 1.4 copy-start.7
  331.8 1.8 copy-start.9
  331.9 2.0 copy-start.28
  336.2 60.4 %all-to-all-start.4 = ((bf16[64,4,2048]{2,1,0:T(4,128)(2,1)}), bf16[64,4,2048]{2,1,0:T(4,128)(2,1)S(1)}, u32[]{:S(2)}, u32[]{:S(2)}) async-start(bf16[64,4,2048]{2,1,0:T(4,128)(2,1)} %reshape.525), calls=%async_computation.4 | async-start | bytes 2097152 | tf_op jit(solution)/shard_map/all_to_all | solution.py:154
  402.1 1.5 copy-start.24
  403.5 1.0 copy-start.3
  403.5 1.1 copy-start.5
  403.5 1.1 copy-start.23
  469.2 4.0 copy-start.8
  482.6 10.7 copy-start.22
  482.6 60.9 %all-to-all-start.1 = ((bf16[64,4,2048]{2,1,0:T(4,128)(2,1)}), bf16[64,4,2048]{2,1,0:T(4,128)(2,1)S(1)}, u32[]{:S(2)}, u32[]{:S(2)}) async-start(bf16[64,4,2048]{2,1,0:T(4,128)(2,1)} %reshape.518), calls=%async_computation.1 | async-start | bytes 2097152 | tf_op jit(solution)/shard_map/all_to_all | solution.py:103
  492.8 340.3 %all-reduce.7.cloned.1.call-start = ((), (), s32[]{:S(2)}) async-start(), calls=%async_computation.6 | async-start | bytes 524288 | tf_op jit(solution)/shard_map/psum | solution.py:167
  494.4 592.7 %collective-permute-start.4 = (bf16[112,2048]{1,0:T(8,128)(2,1)}, bf16[112,2048]{1,0:T(8,128)(2,1)}, u32[]{:S(2)}, u32[]{:S(2)}) collective-permute-start(bf16[112,2048]{1,0:T(8,128)(2,1)} %get-tuple-element.35), channel_id=1, source_target_pairs={{0,384},{128,0},{256,128},{384,256},{1,385},{129,1},{257,129},{385... | collective-permute-start | bytes 1376264 | tf_op jit(solution)/shard_map/ppermute | solution.py:16
  551.2 535.8 %collective-permute-start.3 = (bf16[112,2048]{1,0:T(8,128)(2,1)S(1)}, bf16[112,2048]{1,0:T(8,128)(2,1)S(1)}, u32[]{:S(2)}, u32[]{:S(2)}) collective-permute-start(bf16[112,2048]{1,0:T(8,128)(2,1)S(1)} %fusion.21), channel_id=1, source_target_pairs={{0,128},{128,256},{256,384},{384,0},{1,129},{129,257},{257,385},{3... | collective-permute-start | bytes 1376264 | tf_op jit(solution)/shard_map/ppermute | solution.py:16
Sparse Core Ops, SparseCore 0:
  10.1 26.8 all-gather.6
  39.1 21.3 all-gather.8
  62.6 21.3 all-gather.10
  497.4 335.7 all-reduce.6
where the time goes:
time: 1100 us
  waiting for transfers between devices  549 us (50%)
  blocking collectives  372 us (34%)
  starting transfers between devices  69.6 us (6%)
  local copies, waits for them, and re-layouts  42.3 us (4%)
  other arithmetic  25.2 us (2%)
  matrix products  23.5 us (2%)
  between operations  14.8 us (1%)
    psum x1, waiting for transfers between devices, body(): router_sum, gain_sum = lax.psum((router_term, gain_term), ('expert', 'dp'))  279 us
    psum x1, blocking collectives, body(): router_sum, gain_sum = lax.psum((router_term, gain_term), ('expert', 'dp'))  252 us
    ppermute x3, waiting for transfers between devices, partner_2(): lax.ppermute(shard, axis, [(i, i ^ 1 << stride) for i in range(lax.axis_s...  85.8 us
    all_to_all x1, blocking collectives, body(): lax.all_to_all(send_grads, 'expert', split_axis=0, concat_axis=0, tiled=T...  60.5 us
    all_to_all x1, blocking collectives, body(): lax.all_to_all(send_rows, 'expert', split_axis=0, concat_axis=0, tiled=True)  60.2 us
    all_to_all x1, waiting for transfers between devices, body(): lax.all_to_all(expert_out, 'expert', split_axis=0, concat_axis=0, tiled=T...  49.7 us
    all_to_all x1, waiting for transfers between devices, body(): lax.all_to_all(grad_normed_rows, 'expert', split_axis=0, concat_axis=0, t...  48.8 us
    all_to_all x1, waiting for transfers between devices, body(): lax.all_to_all(output, 'expert', split_axis=0, concat_axis=0, tiled=True)  44.7 us
  transfers between devices with their start and end apart: 13, of which 9 were waited for; matrix products, arithmetic and copies ran while one was open for 3% of the time, Pallas kernels for 0%

commit v1 on v0

--- a/solution.py
+++ b/solution.py
@@ -164,7 +164,7 @@
     )
     router_term = jnp.einsum("te,td->ed", dlogits, normed, preferred_element_type=jnp.float32)
     gain_term = jnp.sum(dnormed * x_float * inv_rms, 0)
-    router_sum, gain_sum = lax.psum((router_term, gain_term), ("expert", "dp"))
+    router_sum, gain_sum = lax.psum(lax.psum((router_term, gain_term), "dp"), "expert")
     blocks = lax.axis_size("expert") * lax.axis_size("dp")
     dxn = dnormed * gain[None, :]
     input_grad = (

time: 1100 us -> 968 us (0.88)
  the two profiles are of different devices: /device:TPU:1 before, /device:TPU:2 now
where the time goes in v1:
time: 968 us; the launch traced here: 960 us
  waiting for transfers between devices  525 us (54%)
  blocking collectives  265 us (27%)
  starting transfers between devices  64.6 us (7%)
  local copies, waits for them, and re-layouts  42.4 us (4%)
  other arithmetic  25.2 us (3%)
  matrix products  23.4 us (2%)
  between operations  14.8 us (2%)
    psum x1, waiting for transfers between devices, body(): lax.psum(lax.psum((router_term, gain_term), 'dp'), 'expert')  247 us
    psum x1, blocking collectives, body(): lax.psum(lax.psum((router_term, gain_term), 'dp'), 'expert')  142 us
    ppermute x3, waiting for transfers between devices, partner_2(): lax.ppermute(shard, axis, [(i, i ^ 1 << stride) for i in range(lax.axis_s...  86.8 us
    all_to_all x1, blocking collectives, body(): lax.all_to_all(send_grads, 'expert', split_axis=0, concat_axis=0, tiled=T...  60.5 us
    all_to_all x1, blocking collectives, body(): lax.all_to_all(send_rows, 'expert', split_axis=0, concat_axis=0, tiled=True)  60.2 us
    all_to_all x1, waiting for transfers between devices, body(): lax.all_to_all(expert_out, 'expert', split_axis=0, concat_axis=0, tiled=T...  53.1 us
    all_to_all x1, waiting for transfers between devices, body(): lax.all_to_all(grad_normed_rows, 'expert', split_axis=0, concat_axis=0, t...  52.2 us
    psum x1, waiting for transfers between devices, body(): lax.psum((router_term, gain_term), 'dp')  42.6 us
  transfers between devices with their start and end apart: 14, of which 10 were waited for; matrix products, arithmetic and copies ran while one was open for 4% of the time, Pallas kernels for 0%

profile of v1, /device:TPU:2, one launch (start us, length us, event | category | flops | bytes accessed | tf_op | source)
XLA Modules:
  0.0 960.2 jit_solution(1757691110487906563)
XLA Ops:
  16.1 1.3 scatter_custom_fusion.1
  17.4 1.4 gather_fusion.3
  19.0 1.3 reshape.523
  20.2 18.7 %all-to-all-start.3 = ((bf16[64,4,2048]{2,1,0:T(4,128)(2,1)}), bf16[64,4,2048]{2,1,0:T(4,128)(2,1)S(1)}, u32[]{:S(2)}, u32[]{:S(2)}) async-start(bf16[64,4,2048]{2,1,0:T(4,128)(2,1)} %reshape.523), calls=%async_computation.3 | async-start | bytes 2097152 | tf_op jit(solution)/shard_map/all_to_all | solution.py:116
  39.7 3.5 collective-permute-start
  43.2 15.0 %all-gather.9.cloned.1.call-done = bf16[1,1,352,2048]{3,2,1,0:T(8,128)(2,1)} async-done(((bf16[1,1,176,2048]{3,2,1,0:T(8,128)(2,1)}), bf16[1,1,352,2048]{3,2,1,0:T(8,128)(2,1)}) %all-gather.9.cloned.1.call-update) | async-done | bytes 1441808 | tf_op jit(solution)/shard_map/all_gather | solution.py:70
  58.2 3.5 collective-permute-start.1
  61.7 20.1 %all-gather.11.cloned.1.call-done = bf16[1,1,352,2048]{3,2,1,0:T(8,128)(2,1)} async-done(((bf16[1,1,176,2048]{3,2,1,0:T(8,128)(2,1)}), bf16[1,1,352,2048]{3,2,1,0:T(8,128)(2,1)}) %all-gather.11.cloned.1.call-update) | async-done | bytes 1441808 | tf_op jit(solution)/shard_map/all_gather | solution.py:71
  81.8 3.5 collective-permute-start.2
  85.2 32.3 %collective-permute-done = bf16[352,2048]{1,0:T(8,128)(2,1)} collective-permute-done((bf16[352,2048]{1,0:T(8,128)(2,1)}, bf16[352,2048]{1,0:T(8,128)(2,1)}, u32[]{:S(2)}, u32[]{:S(2)}) %collective-permute-start) | collective-permute-done | bytes 1441824 | tf_op jit(solution)/shard_map/ppermute | solution.py:10
  117.6 3.1 select_bitcast_fusion.5
  120.7 27.8 %collective-permute-done.1 = bf16[352,2048]{1,0:T(8,128)(2,1)} collective-permute-done((bf16[352,2048]{1,0:T(8,128)(2,1)}, bf16[352,2048]{1,0:T(8,128)(2,1)}, u32[]{:S(2)}, u32[]{:S(2)}) %collective-permute-start.1) | collective-permute-done | bytes 1441824 | tf_op jit(solution)/shard_map/ppermute | solution.py:10
  148.5 3.2 select_bitcast_fusion.3
  151.6 26.7 %collective-permute-done.2 = bf16[352,2048]{1,0:T(8,128)(2,1)} collective-permute-done((bf16[352,2048]{1,0:T(8,128)(2,1)}, bf16[352,2048]{1,0:T(8,128)(2,1)}, u32[]{:S(2)}, u32[]{:S(2)}) %collective-permute-start.2) | collective-permute-done | bytes 1441824 | tf_op jit(solution)/shard_map/ppermute | solution.py:10
  178.3 3.1 select_bitcast_fusion.1
  181.4 1.1 reshape.624
  182.5 2.8 fusion.45
  185.4 0.9 fusion.43
  187.7 1.1 fusion.3
  188.8 1.2 reshape.527
  190.0 14.7 %all-to-all-start.5 = ((bf16[64,4,2048]{2,1,0:T(4,128)(2,1)}), bf16[64,4,2048]{2,1,0:T(4,128)(2,1)S(1)}, u32[]{:S(2)}, u32[]{:S(2)}) async-start(bf16[64,4,2048]{2,1,0:T(4,128)(2,1)} %reshape.527), calls=%async_computation.5 | async-start | bytes 2097152 | tf_op jit(solution)/shard_map/all_to_all | solution.py:118
  205.2 53.1 %all-to-all-done.5 = bf16[64,4,2048]{2,1,0:T(4,128)(2,1)S(1)} async-done(((bf16[64,4,2048]{2,1,0:T(4,128)(2,1)}), bf16[64,4,2048]{2,1,0:T(4,128)(2,1)S(1)}, u32[]{:S(2)}, u32[]{:S(2)}) %all-to-all-start.5) | async-done | bytes 1048608 | tf_op jit(solution)/shard_map/all_to_all | solution.py:118
  258.7 1.3 gather_fusion.5
  259.9 1.4 select_convert_fusion
  261.3 2.4 reshape.537
  263.7 1.4 fusion.96
  266.6 0.9 copy.28
  268.0 1.4 gather_fusion
  270.4 60.5 %all_to_all.30 = bf16[64,4,2048]{2,1,0:T(4,128)(2,1)S(1)} all-to-all(bf16[64,4,2048]{2,1,0:T(4,128)(2,1)S(1)} %broadcast_select_fusion.2), channel_id=1, replica_groups=mesh['segment'=4,'expert'=64,'dp'=2] {'expert'}, dimensions={0} | all-to-all | bytes 2097152 | tf_op jit(solution)/shard_map/all_to_all | solution.py:136
  330.9 1.1 reshape.623
  332.0 2.8 fusion.42
  334.8 1.1 convolution_bitcast_fusion.1
  336.8 1.1 fusion.1
  337.9 1.3 reshape.525
  339.2 6.8 all-to-all-start.4
  346.0 1.4 scatter_custom_fusion
  347.5 52.2 %all-to-all-done.4 = bf16[64,4,2048]{2,1,0:T(4,128)(2,1)S(1)} async-done(((bf16[64,4,2048]{2,1,0:T(4,128)(2,1)}), bf16[64,4,2048]{2,1,0:T(4,128)(2,1)S(1)}, u32[]{:S(2)}, u32[]{:S(2)}) %all-to-all-start.4) | async-done | bytes 1048608 | tf_op jit(solution)/shard_map/all_to_all | solution.py:154
  400.0 1.3 gather_fusion.4
  401.2 1.5 select_convert_fusion.1
  402.7 2.4 reshape.536
  405.1 1.4 fusion.95
  407.7 1.2 fusion.29
  408.9 1.4 gather_fusion.1
  410.9 60.2 %all_to_all.31 = bf16[64,4,2048]{2,1,0:T(4,128)(2,1)S(1)} all-to-all(bf16[64,4,2048]{2,1,0:T(4,128)(2,1)S(1)} %reshape.516), channel_id=1, replica_groups=mesh['segment'=4,'expert'=64,'dp'=2] {'expert'}, dimensions={0} | all-to-all | bytes 2097152 | tf_op jit(solution)/shard_map/all_to_all | solution.py:101
  471.1 1.2 reshape.621
  472.3 4.0 fusion.44
  476.3 7.0 fusion.2
  483.4 2.2 reshape.518
  485.6 6.9 all-to-all-start.1
  493.0 1.0 fusion.61
  494.1 42.6 %all-reduce.8.cloned.1.call-done = f32[32,2048]{1,0:T(8,128)} async-done(((f32[32,2048]{1,0:T(8,128)}), f32[32,2048]{1,0:T(8,128)}) %all-reduce.8.cloned.1.call-update) | async-done | bytes 262160 | tf_op jit(solution)/shard_map/psum | solution.py:167
  536.7 3.5 collective-permute-start.4
  540.2 6.0 all-to-all-done.1
  546.5 1.3 gather_fusion.2
  547.7 1.5 select_convert_fusion.2
  549.2 2.4 reshape.531
  551.6 1.4 fusion.97
  553.0 0.9 fusion.21
  553.9 3.4 collective-permute-start.3
  557.3 247.1 %all-reduce.10.cloned.1.call-done = f32[32,2048]{1,0:T(8,128)} async-done(((f32[32,2048]{1,0:T(8,128)}), f32[32,2048]{1,0:T(8,128)}) %all-reduce.10.cloned.1.call-update) | async-done | bytes 262160 | tf_op jit(solution)/shard_map/psum | solution.py:167
  804.4 1.7 multiply_bitcast_fusion
  806.1 2.5 psum.30
  808.5 141.7 %psum.31 = f32[2048]{0:T(1024)S(1)} all-reduce(f32[2048]{0:T(1024)S(1)} %psum.30), channel_id=1, replica_groups=mesh['segment'=4,'expert'=64,'dp'=2] {'expert'}, use_global_device_ids=true, to_apply=%region_19.22 | all-reduce | flops 2048 | bytes 16384 | tf_op jit(solution)/shard_map/psum | solution.py:167
  951.6 1.8 copy.75
  (144 shorter events, 19.7 us)
Async XLA Ops:
  7.2 197.7 %copy-start = (bf16[1,32,2048]{2,1,0:T(8,128)(2,1)S(1)}, bf16[1,32,2048]{2,1,0:T(8,128)(2,1)}, u32[]{:S(2)}) copy-start(bf16[1,32,2048]{2,1,0:T(8,128)(2,1)} %param.20) | copy-start | bytes 393220
  7.2 7.2 copy-start.2
  7.2 7.4 copy-start.1
  7.2 8.1 copy-start.20
  7.2 32.5 %all-gather.7.cloned.1.call-start = ((), (), s32[]{:S(2)}) async-start(), calls=%async_computation.8 | async-start | bytes 2162688 | tf_op jit(solution)/shard_map/all_gather | solution.py:69
  7.9 50.3 %all-gather.9.cloned.1.call-start = ((), (), s32[]{:S(2)}) async-start(), calls=%async_computation.9 | async-start | bytes 2162688 | tf_op jit(solution)/shard_map/all_gather | solution.py:70
  20.2 161.2 %all-to-all-start.3 = ((bf16[64,4,2048]{2,1,0:T(4,128)(2,1)}), bf16[64,4,2048]{2,1,0:T(4,128)(2,1)S(1)}, u32[]{:S(2)}, u32[]{:S(2)}) async-start(bf16[64,4,2048]{2,1,0:T(4,128)(2,1)} %reshape.523), calls=%async_computation.3 | async-start | bytes 2097152 | tf_op jit(solution)/shard_map/all_to_all | solution.py:116
  39.0 42.8 %all-gather.11.cloned.1.call-start = ((), (), s32[]{:S(2)}) async-start(), calls=%async_computation.10 | async-start | bytes 2162688 | tf_op jit(solution)/shard_map/all_gather | solution.py:71
  39.7 77.8 %collective-permute-start = (bf16[352,2048]{1,0:T(8,128)(2,1)}, bf16[352,2048]{1,0:T(8,128)(2,1)}, u32[]{:S(2)}, u32[]{:S(2)}) collective-permute-start(bf16[352,2048]{1,0:T(8,128)(2,1)} %bitcast.208), channel_id=1, source_target_pairs={{0,2},{2,0},{4,6},{6,4},{8,10},{10,8},{12,14},{14,12},{16,18},{18,... | collective-permute-start | bytes 4325384 | tf_op jit(solution)/shard_map/ppermute | solution.py:10
  58.2 90.2 %collective-permute-start.1 = (bf16[352,2048]{1,0:T(8,128)(2,1)}, bf16[352,2048]{1,0:T(8,128)(2,1)}, u32[]{:S(2)}, u32[]{:S(2)}) collective-permute-start(bf16[352,2048]{1,0:T(8,128)(2,1)} %bitcast.209), channel_id=1, source_target_pairs={{0,2},{2,0},{4,6},{6,4},{8,10},{10,8},{12,14},{14,12},{16,18},{18,... | collective-permute-start | bytes 4325384 | tf_op jit(solution)/shard_map/ppermute | solution.py:10
  81.8 96.5 %collective-permute-start.2 = (bf16[352,2048]{1,0:T(8,128)(2,1)}, bf16[352,2048]{1,0:T(8,128)(2,1)}, u32[]{:S(2)}, u32[]{:S(2)}) collective-permute-start(bf16[352,2048]{1,0:T(8,128)(2,1)} %bitcast.210), channel_id=1, source_target_pairs={{0,2},{2,0},{4,6},{6,4},{8,10},{10,8},{12,14},{14,12},{16,18},{18,... | collective-permute-start | bytes 4325384 | tf_op jit(solution)/shard_map/ppermute | solution.py:10
  85.2 63.2 %copy-start.17 = (bf16[1,1,352,2048]{3,2,1,0:T(8,128)(2,1)S(1)}, bf16[1,1,352,2048]{3,2,1,0:T(8,128)(2,1)}, u32[]{:S(2)}) copy-start(bf16[1,1,352,2048]{3,2,1,0:T(8,128)(2,1)} %all-gather.9.cloned.1.call-done) | copy-start | bytes 4325380
  120.7 61.9 %copy-start.6 = (bf16[1,352,2048]{2,1,0:T(8,128)(2,1)}, bf16[1,352,2048]{2,1,0:T(8,128)(2,1)S(1)}, u32[]{:S(2)}) copy-start(bf16[1,352,2048]{2,1,0:T(8,128)(2,1)S(1)} %get-tuple-element.21) | copy-start | bytes 4325380
  120.7 57.6 %copy-start.18 = (bf16[1,1,352,2048]{3,2,1,0:T(8,128)(2,1)S(1)}, bf16[1,1,352,2048]{3,2,1,0:T(8,128)(2,1)}, u32[]{:S(2)}) copy-start(bf16[1,1,352,2048]{3,2,1,0:T(8,128)(2,1)} %all-gather.11.cloned.1.call-done) | copy-start | bytes 4325380
  182.5 2.8 copy-start.10
  182.5 2.8 copy-start.12
  182.5 2.8 copy-start.19
  185.3 1.0 copy-start.25
  185.4 1.6 copy-start.14
  185.4 2.3 copy-start.16
  186.4 2.4 copy-start.27
  190.0 15.2 %copy-start.21 = (s32[1,112,2]{1,2,0:T(2,128)S(1)}, s32[1,112,2]{1,2,0:T(2,128)}, u32[]{:S(2)}) copy-start(s32[1,112,2]{1,2,0:T(2,128)} %param.18) | copy-start | bytes 2692
  190.0 68.4 %all-to-all-start.5 = ((bf16[64,4,2048]{2,1,0:T(4,128)(2,1)}), bf16[64,4,2048]{2,1,0:T(4,128)(2,1)S(1)}, u32[]{:S(2)}, u32[]{:S(2)}) async-start(bf16[64,4,2048]{2,1,0:T(4,128)(2,1)} %reshape.527), calls=%async_computation.5 | async-start | bytes 2097152 | tf_op jit(solution)/shard_map/all_to_all | solution.py:118
  263.7 1.4 copy-start.4
  270.4 61.6 %copy-start.15 = (bf16[1,352,2048]{2,1,0:T(8,128)(2,1)S(1)}, bf16[1,352,2048]{2,1,0:T(8,128)(2,1)}, u32[]{:S(2)}) copy-start(bf16[1,352,2048]{2,1,0:T(8,128)(2,1)} %get-tuple-element.25) | copy-start | bytes 4325380
  332.0 2.8 copy-start.11
  332.0 2.8 copy-start.13
  332.0 2.8 copy-start.26
  334.8 1.4 copy-start.7
  334.8 1.8 copy-start.9
  334.8 2.0 copy-start.28
  339.2 60.5 %all-to-all-start.4 = ((bf16[64,4,2048]{2,1,0:T(4,128)(2,1)}), bf16[64,4,2048]{2,1,0:T(4,128)(2,1)S(1)}, u32[]{:S(2)}, u32[]{:S(2)}) async-start(bf16[64,4,2048]{2,1,0:T(4,128)(2,1)} %reshape.525), calls=%async_computation.4 | async-start | bytes 2097152 | tf_op jit(solution)/shard_map/all_to_all | solution.py:154
  405.1 1.5 copy-start.24
  406.5 1.0 copy-start.3
  406.5 1.1 copy-start.5
  406.6 1.1 copy-start.23
  472.3 4.0 copy-start.8
  485.6 7.3 copy-start.22
  485.6 60.6 %all-to-all-start.1 = ((bf16[64,4,2048]{2,1,0:T(4,128)(2,1)}), bf16[64,4,2048]{2,1,0:T(4,128)(2,1)S(1)}, u32[]{:S(2)}, u32[]{:S(2)}) async-start(bf16[64,4,2048]{2,1,0:T(4,128)(2,1)} %reshape.518), calls=%async_computation.1 | async-start | bytes 2097152 | tf_op jit(solution)/shard_map/all_to_all | solution.py:103
  492.5 44.2 %all-reduce.8.cloned.1.call-start = ((), (), s32[]{:S(2)}) async-start(), calls=%async_computation.6 | async-start | bytes 524288 | tf_op jit(solution)/shard_map/psum | solution.py:167
  494.0 310.4 %all-reduce.10.cloned.1.call-start = ((), (), s32[]{:S(2)}) async-start(), calls=%async_computation.7 | async-start | bytes 524288 | tf_op jit(solution)/shard_map/psum | solution.py:167
  536.7 414.1 %collective-permute-start.4 = (bf16[112,2048]{1,0:T(8,128)(2,1)}, bf16[112,2048]{1,0:T(8,128)(2,1)}, u32[]{:S(2)}, u32[]{:S(2)}) collective-permute-start(bf16[112,2048]{1,0:T(8,128)(2,1)} %get-tuple-element.35), channel_id=1, source_target_pairs={{0,384},{128,0},{256,128},{384,256},{1,385},{129,1},{257,129},{385... | collective-permute-start | bytes 1376264 | tf_op jit(solution)/shard_map/ppermute | solution.py:16
  553.9 396.9 %collective-permute-start.3 = (bf16[112,2048]{1,0:T(8,128)(2,1)S(1)}, bf16[112,2048]{1,0:T(8,128)(2,1)S(1)}, u32[]{:S(2)}, u32[]{:S(2)}) collective-permute-start(bf16[112,2048]{1,0:T(8,128)(2,1)S(1)} %fusion.21), channel_id=1, source_target_pairs={{0,128},{128,256},{256,384},{384,0},{1,129},{129,257},{257,385},{3... | collective-permute-start | bytes 1376264 | tf_op jit(solution)/shard_map/ppermute | solution.py:16
Sparse Core Ops, SparseCore 0:
  10.1 24.5 all-gather.6
  36.8 21.3 all-gather.8
  60.3 21.3 all-gather.10
  496.5 40.1 all-reduce.7
  540.4 263.9 all-reduce.9
